TPU v7x, 512 devices: a whole 4x8x8 slice. The times are simulated.
512 devices in a mesh: tok: 16 (over z, y_hi), hid: 32 (over y_lo, x, core).
Axes of the slice: x: 4, y: 8 (y_hi: 2, y_lo: 4; y = y_hi * 4 + y_lo), z: 8, core: 2. Of those that a mesh axis runs over, the one named last changes fastest.
Arguments:
- resid_in: bfloat16 [512, 8192], P('hid', 'tok'), may hold values from -64 to 64
- norm_gain: float32 [8192], P('tok'), may hold values from 0.1 to 1.9
- gate_weight: bfloat16 [8192, 28672], P('tok', 'hid'), may hold values from -0.0625 to 0.0625
- up_weight: bfloat16 [8192, 28672], P('tok', 'hid'), may hold values from -0.0625 to 0.0625
- down_weight: bfloat16 [28672, 8192], P('hid', 'tok'), may hold values from -0.0625 to 0.0625
- labels: int32 [512], replicated, may hold values from 0 to 63
Outputs:
- gram: float32 [8192, 8192], P(('tok', 'hid'))
- cross: float32 [8192, 64], P(('tok', 'hid'))
All inputs are finite; a program needn't handle non-finite values.
Results may differ from a plain program's by a relative error of at most 0.014.
Values may be sent and summed in bfloat16 or wider, within the bound.
A program may use at most 64 MiB of HBM per device.

v0:
```python
import jax
import jax.numpy as jnp
from jax import lax
from jax.sharding import PartitionSpec as P

D = 8192
CLASSES = 64


def on_device(resid_in, norm_gain, gate_weight, up_weight, down_weight, labels):
    gathered = lax.all_gather(resid_in, "hid", axis=0, tiled=True)
    xf = gathered.astype(jnp.float32)
    local_sq = jnp.sum(xf * xf, axis=1)
    total_sq = lax.psum(local_sq, "tok")
    scale_rows = lax.rsqrt(total_sq / float(D) + 1e-05)
    normed = (xf * scale_rows[:, None] * norm_gain[None, :]).astype(jnp.bfloat16)
    both_weights = jnp.concatenate([gate_weight, up_weight], axis=1)
    shard_ff = gate_weight.shape[1]
    paired = lax.psum_scatter(
        jnp.dot(normed, both_weights, preferred_element_type=jnp.float32).astype(jnp.bfloat16),
        "tok",
        scatter_dimension=0,
        tiled=True,
    ).astype(jnp.float32)
    hidden = (jax.nn.silu(paired[:, :shard_ff]) * paired[:, shard_ff:]).astype(jnp.bfloat16)
    partial_out = jnp.dot(
        lax.all_gather(hidden, "tok", axis=0, tiled=True),
        down_weight,
        preferred_element_type=jnp.float32,
    )
    ntok = xf.shape[0]
    panel = xf.shape[1] // lax.axis_size("hid")
    offset = lax.axis_index("hid") * panel
    summed = lax.psum_scatter(
        partial_out.astype(jnp.bfloat16), "hid", scatter_dimension=1, tiled=True
    ).astype(jnp.float32)
    x_cols = lax.dynamic_slice_in_dim(xf, offset, panel, 1)
    resid_cols = (x_cols + summed).astype(jnp.bfloat16)
    prod = lax.dot_general(
        resid_cols,
        lax.all_gather(resid_cols, ("tok", "hid"), axis=1, tiled=True),
        (((0,), (0,)), ((), ())),
        preferred_element_type=jnp.float32,
    )
    gram = prod / float(ntok)
    onehot = (labels[:, None] == jnp.arange(CLASSES, dtype=jnp.int32)[None, :]).astype(jnp.bfloat16)
    counts = jnp.sum(onehot.astype(jnp.float32), axis=0)
    class_sums = lax.dot_general(
        resid_cols, onehot, (((0,), (0,)), ((), ())), preferred_element_type=jnp.float32
    )
    cross = class_sums / jnp.maximum(counts, 1.0)[None, :]
    return (gram, cross)


def solution(mesh):
    return jax.shard_map(
        on_device,
        mesh=mesh,
        in_specs=(
            P("hid", "tok"),
            P("tok"),
            P("tok", "hid"),
            P("tok", "hid"),
            P("hid", "tok"),
            P(),
        ),
        out_specs=(P(("tok", "hid"), None), P(("tok", "hid"), None)),
        check_vma=False,
    )
```

profile of v0, /device:TPU:1, one launch (start us, length us, event | category | flops | bytes accessed | tf_op | source)
XLA Modules:
  0.0 691.0 jit_solution(11875496450596271961)
XLA Ops:
  7.2 0.0 copy-start
  7.2 0.0 reduce-scatter.3.cloned.1.call-start
  7.2 46.5 %all_gather.9 = bf16[512,512]{1,0:T(8,128)(2,1)S(1)} all-gather(bf16[16,512]{1,0:T(8,128)(2,1)} %param.6), channel_id=1, replica_groups=mesh['tok'=16,'hid'=32] {'hid'}, dimensions={0}, use_global_device_ids=true | all-gather | bytes 540672 | tf_op jit(solution)/shard_map/all_gather | solution.py:11
  53.7 0.2 copy.10
  53.9 0.2 multiply_reduce_fusion
  54.1 50.9 %psum.7 = f32[512]{0:T(512)S(1)} all-reduce(f32[512]{0:T(512)S(1)} %multiply_reduce_fusion), channel_id=1, replica_groups=mesh['tok'=16,'hid'=32] {'tok'}, use_global_device_ids=true, to_apply=%region_1.0 | all-reduce | flops 512 | bytes 4096 | tf_op jit(solution)/shard_map/psum | solution.py:14
  105.0 4.0 convolution_convert_fusion
  109.0 0.0 reduce-scatter.3.cloned.1.call-update
  109.0 0.0 copy-start.1
  109.0 0.0 reduce-scatter.5.cloned.1.call-start
  109.0 217.4 %reduce-scatter.3.cloned.1.call-done = bf16[32,1792]{1,0:T(8,128)(2,1)} async-done(((bf16[512,1792]{1,0:T(8,128)(2,1)}), bf16[32,1792]{1,0:T(8,128)(2,1)}) %reduce-scatter.3.cloned.1.call-update) | async-done | bytes 114704 | tf_op jit(solution)/shard_map/reduce_scatter | solution.py:19
  326.4 0.9 convert_element_type.33
  327.4 57.8 %all_gather.10 = bf16[512,896]{1,0:T(8,128)(2,1)S(1)} all-gather(bf16[32,896]{1,0:T(8,128)(2,1)S(1)} %fusion.7), channel_id=1, replica_groups=mesh['tok'=16,'hid'=32] {'tok'}, dimensions={0}, use_global_device_ids=true | all-gather | bytes 974848 | tf_op jit(solution)/shard_map/all_gather | solution.py:27
  385.2 0.0 copy-done
  385.2 1.6 convolution_convert_fusion.1
  386.7 0.0 reduce-scatter.5.cloned.1.call-update
  386.7 0.0 all-gather.2.cloned.1.call-start
  386.8 0.1 convert_element_type.30
  386.9 157.9 %reduce-scatter.5.cloned.1.call-done = bf16[512,16]{0,1:T(8,128)(2,1)} async-done(((bf16[512,512]{0,1:T(8,128)(2,1)}), bf16[512,16]{0,1:T(8,128)(2,1)}) %reduce-scatter.5.cloned.1.call-update) | async-done | bytes 16400 | tf_op jit(solution)/shard_map/reduce_scatter | solution.py:34
  544.9 1.3 add_convert_fusion
  546.2 0.0 all-gather.2.cloned.1.call-update
  546.2 0.0 copy-done.1
  546.2 0.1 convert_reduce_fusion
  546.3 1.5 convolution_divide_fusion
  547.8 130.1 %all-gather.2.cloned.1.call-done = bf16[512,8192]{0,1:T(8,128)(2,1)} async-done(((bf16[512,16]{0,1:T(8,128)(2,1)}), bf16[512,8192]{0,1:T(8,128)(2,1)}) %all-gather.2.cloned.1.call-update) | async-done | bytes 8388624 | tf_op jit(solution)/shard_map/all_gather | solution.py:41
  677.9 6.5 convolution_multiply_fusion
  (3 shorter events, 0.1 us)
Async XLA Ops:
  7.2 378.0 %copy-start = (bf16[896,512]{1,0:T(8,128)(2,1)S(1)}, bf16[896,512]{1,0:T(8,128)(2,1)}, u32[]{:S(2)}) copy-start(bf16[896,512]{1,0:T(8,128)(2,1)} %param.10) | copy-start | bytes 2752516
  7.2 319.2 %reduce-scatter.3.cloned.1.call-start = ((), (), s32[]{:S(2)}) async-start(), calls=%async_computation.2 | async-start | bytes 1949696 | tf_op jit(solution)/shard_map/reduce_scatter | solution.py:19
  109.0 437.2 %copy-start.1 = (s32[512]{0:T(512)S(1)}, s32[512]{0:T(512)}, u32[]{:S(2)}) copy-start(s32[512]{0:T(512)} %param.11) | copy-start | bytes 6148
  109.0 435.9 %reduce-scatter.5.cloned.1.call-start = ((), (), s32[]{:S(2)}) async-start(), calls=%async_computation.3 | async-start | bytes 540672 | tf_op jit(solution)/shard_map/reduce_scatter | solution.py:34
  386.7 291.2 %all-gather.2.cloned.1.call-start = ((), (), s32[]{:S(2)}) async-start(), calls=%async_computation.4 | async-start | bytes 8404992 | tf_op jit(solution)/shard_map/all_gather | solution.py:41
Sparse Core Ops, SparseCore 0:
  109.1 217.2 reduce-scatter.2
  386.9 157.9 reduce-scatter.4
  549.3 128.5 all-gather.1
where the time goes:
time: 691 us
  waiting for transfers between devices  505 us (73%)
  blocking collectives  155 us (22%)
  between operations  13.8 us (2%)
  matrix products  13.5 us (2%)
    reduce_scatter x1, waiting for transfers between devices, on_device(): lax.psum_scatter(jnp.dot(normed, both_weights, preferred_element_type=jnp...  217 us
    reduce_scatter x1, waiting for transfers between devices, on_device(): lax.psum_scatter(partial_out.astype(jnp.bfloat16), 'hid', scatter_dimensi...  158 us
    all_gather x1, waiting for transfers between devices, on_device(): lax.all_gather(resid_cols, ('tok', 'hid'), axis=1, tiled=True)  130 us
    all_gather x1, blocking collectives, on_device(): lax.all_gather(hidden, 'tok', axis=0, tiled=True)  57.8 us
    psum x1, blocking collectives, on_device(): total_sq = lax.psum(local_sq, 'tok')  50.9 us
    all_gather x1, blocking collectives, on_device(): gathered = lax.all_gather(resid_in, 'hid', axis=0, tiled=True)  46.5 us
  transfers between devices with their start and end apart: 3, of which 3 were waited for; matrix products, arithmetic and copies ran while one was open for 0% of the time, Pallas kernels for 0%

commit v1 on v0

v1 whole, which is shorter than its diff:
```python
import jax
import jax.numpy as jnp
from jax import lax
from jax.experimental import pallas as pl
from jax.experimental.pallas import tpu as pltpu
from jax.sharding import PartitionSpec as P

CLASSES = 64
EPS = 1e-05
F32 = jnp.float32
BF16 = jnp.bfloat16
MESH = pl.DeviceIdType.MESH
NT = (((1,), (1,)), ((), ()))


def kernel(x_ref, gain_ref, wg_hbm, wu_hbm, wd_hbm, lab_ref, gram_ref, cross_ref,
           xg, xn, wg, wu, wd, wdt, sqb, sqz, sqp, cown, csend, crecv, fin, ysend, yrecv,
           hb, ot, es, er, ea, ex, exr, ey, eyr, cb, rb, gt, gr,
           wsem, a_s, a_r, q_s, q_r, c_s, c_r, y_s, y_r, d_s, d_r, e_s, e_r, f_s, f_r):
    t = lax.axis_index("tok")
    h = lax.axis_index("hid")
    z, yh = t // 2, lax.rem(t, 2)
    yl, x, c = h // 8, lax.rem(h // 2, 4), lax.rem(h, 2)
    y = yh * 4 + yl

    def at(z=z, y=y, x=x, c=c):
        return {"tok": z * 2 + y // 4, "hid": (lax.rem(y, 4) * 4 + x) * 2 + c}

    def zp(d):
        return at(z=lax.rem(z + d + 8, 8))

    def yp(d):
        return at(y=lax.rem(y + d + 8, 8))

    def ylp(d):
        return at(y=yh * 4 + lax.rem(yl + d, 4))

    def xp(d):
        return at(x=lax.rem(x + d, 4))

    sib = at(c=1 - c)
    part = yp(4)

    loads = [pltpu.make_async_copy(a, b, wsem.at[i])
             for i, (a, b) in enumerate(((wg_hbm, wg), (wu_hbm, wu), (wd_hbm, wd)))]
    for cp in loads:
        cp.start()

    barrier = pltpu.get_barrier_semaphore()
    peers = [zp(d) for d in range(1, 8)] + [yp(d) for d in range(1, 8)]
    peers += [xp(d) for d in range(1, 4)] + [sib]
    for p in peers:
        pl.semaphore_signal(barrier, inc=1, device_id=p, device_id_type=MESH)
    xg[yl, x, c] = x_ref[...]
    pl.semaphore_wait(barrier, len(peers))

    sends = []

    def rcopy(src, dst, ss, rs, dev):
        cp = pltpu.make_async_remote_copy(src_ref=src, dst_ref=dst, send_sem=ss, recv_sem=rs,
                                          device_id=dev, device_id_type=MESH)
        cp.start()
        return cp

    def put(src, dst, ss, rs, dev):
        cp = rcopy(src, dst, ss, rs, dev)
        sends.append(cp)
        return cp

    cps = [put(xg.at[yl, x, c], xg.at[yl, x, c], a_s.at[d - 1], a_r.at[d - 1], ylp(d)) for d in (1, 2, 3)]
    for cp in cps:
        cp.wait_recv()
    cps = [put(xg.at[:, x, c], xg.at[:, x, c], a_s.at[d + 2], a_r.at[d + 2], xp(d)) for d in (1, 2, 3)]
    for cp in cps:
        cp.wait_recv()
    cp = put(xg.at[:, :, c], xg.at[:, :, c], a_s.at[6], a_r.at[6], sib)
    cp.wait_recv()

    xa = xg[...].reshape(512, 512)
    xf = xa.astype(F32)
    xn[...] = (xf * gain_ref[...]).astype(BF16)
    for cp in loads:
        cp.wait()

    def own(q, sub):
        rows = xn[pl.ds(pl.multiple_of(q * 64 + sub * 32, 32), 32), :]
        cown[sub, 0] = jnp.dot(rows, wg[...], preferred_element_type=F32)
        cown[sub, 1] = jnp.dot(rows, wu[...], preferred_element_type=F32)

    right, left = zp(1), zp(-1)
    streams = [(0, 0), (1, 0), (0, 1), (1, 1)]

    def ring(k, s):
        sub, half = s
        return pltpu.make_async_remote_copy(
            src_ref=csend.at[k, sub, half], dst_ref=crecv.at[k, sub, half],
            send_sem=c_s.at[k, sub, half], recv_sem=c_r.at[k, sub, half],
            device_id=right if sub == 0 else left, device_id_type=MESH)

    def owns(k):
        own(lax.rem(z + 15 - k, 8), 0)
        own(lax.rem(z + 1 + k, 8), 1)

    owns(0)
    for s in streams:
        csend[0, s[0], s[1]] = cown[s[0], s[1]].astype(BF16)
        ring(0, s).start()

    x2 = xf * xf
    hi = x2.astype(BF16)
    lo = (x2 - hi.astype(F32)).astype(BF16)
    ones = jnp.ones((8, 512), BF16)
    sq = (lax.dot_general(ones, hi, NT, preferred_element_type=F32)
          + lax.dot_general(ones, lo, NT, preferred_element_type=F32))
    sqb[...] = jnp.zeros_like(sqb)
    for k in range(4):
        sqb[k:k + 1, :] = sq[0:1, k * 128:(k + 1) * 128]
    qcps = [put(sqb, sqz.at[d - 1], q_s.at[d - 1], q_r.at[d - 1], zp(d)) for d in range(1, 8)]

    def step(k, _):
        owns(k)
        for s in streams:
            ring(k - 1, s).wait_recv()
            csend[k, s[0], s[1]] = (cown[s[0], s[1]] + crecv[k - 1, s[0], s[1]].astype(F32)).astype(BF16)
            ring(k, s).start()
        return 0

    lax.fori_loop(1, 7, step, 0)

    own(z, 0)
    own(z, 1)
    for cp in qcps:
        cp.wait_recv()
    tot = sqb[...]
    for d in range(7):
        tot = tot + sqz[d]
    sqp[0] = tot
    qy = put(sqp.at[0], sqp.at[1], q_s.at[7], q_r.at[7], part)
    wdt[...] = wd[...].T
    sel = (lax.broadcasted_iota(jnp.int32, (16, 512), 1)
           == lax.broadcasted_iota(jnp.int32, (16, 512), 0) + h * 16).astype(BF16)
    xcols = lax.dot_general(sel, xa, NT, preferred_element_type=F32)
    onehot = (lax.broadcasted_iota(jnp.int32, (CLASSES, 512), 0) == lab_ref[...]).astype(BF16)
    counts = lax.dot_general(ones, onehot, NT, preferred_element_type=F32)
    qy.wait_recv()
    tot = sqp[0] + sqp[1]
    tix = (lax.broadcasted_iota(jnp.int32, (64, 128), 0) + z * 64
           - lax.broadcasted_iota(jnp.int32, (64, 128), 1))
    pick = jnp.zeros((64, 128), F32)
    for k in range(4):
        pick = pick + jnp.where(tix == k * 128, tot[k:k + 1, :], 0.0)
    scale = lax.rsqrt(jnp.sum(pick, axis=1, keepdims=True) / 8192.0 + EPS)

    ycps = []
    for s in streams:
        sub, half = s
        ring(6, s).wait_recv()
        v = cown[sub, half] + crecv[6, sub, half].astype(F32)
        fin[sub, half] = v
        ysend[sub, half] = v.astype(BF16)
        ycps.append(put(ysend.at[sub, half], yrecv.at[sub, half], y_s.at[sub, half], y_r.at[sub, half], part))
    for cp in ycps:
        cp.wait_recv()
    for sub in range(2):
        sc = scale[sub * 32:(sub + 1) * 32, :]
        gate = (fin[sub, 0] + yrecv[sub, 0].astype(F32)) * sc
        up = (fin[sub, 1] + yrecv[sub, 1].astype(F32)) * sc
        hb[z, sub] = (gate / (1.0 + jnp.exp(-gate)) * up).astype(BF16)

    def dput(k, way, sub):
        q = lax.rem(z + 8 - k, 8) if way == 0 else lax.rem(z + k, 8)
        return put(hb.at[q, sub], hb.at[q, sub], d_s.at[k, way, sub], d_r.at[k, way, sub],
                   right if way == 0 else left)

    live = {}
    for sub in range(2):
        for way in range(2):
            live[way, sub] = dput(0, way, sub)
    for k in range(1, 4):
        for sub in range(2):
            for way in range(2):
                live[way, sub].wait_recv()
                if k < 3 or way == sub:
                    live[way, sub] = dput(k, way, sub)
    live[0, 0].wait_recv()
    live[1, 1].wait_recv()

    hall = hb[...].reshape(512, 896)
    ot[...] = lax.dot_general(wdt[...], hall, NT, preferred_element_type=F32).reshape(4, 4, 2, 16, 512)

    es[...] = ot[:, :, 1 - c].astype(BF16)
    cp = put(es, er, e_s.at[0], e_r.at[0], sib)
    cp.wait_recv()
    v = ot[:, :, c] + er[...].astype(F32)
    ea[...] = v
    ex[...] = v.astype(BF16)
    cps = [put(ex.at[:, lax.rem(x + d, 4)], exr.at[d - 1], e_s.at[d], e_r.at[d], xp(d)) for d in (1, 2, 3)]
    for cp in cps:
        cp.wait_recv()
    v = ea[:, x]
    for d in range(3):
        v = v + exr[d].astype(F32)
    ea[:, 0] = v
    ey[...] = v.astype(BF16)
    cps = [put(ey.at[lax.rem(yl + d, 4)], eyr.at[d - 1], e_s.at[d + 3], e_r.at[d + 3], ylp(d)) for d in (1, 2, 3)]
    for cp in cps:
        cp.wait_recv()
    m = ea[yl, 0]
    for d in range(3):
        m = m + eyr[d].astype(F32)
    r = (xcols + m).astype(BF16)

    cb[z, x, c] = r
    rb[y] = r
    zc = [put(cb.at[z, x, c], cb.at[z, x, c], f_s.at[d - 1], f_r.at[d - 1], zp(d)) for d in range(1, 8)]
    yc = [put(cb.at[z, x, c], rb.at[y], f_s.at[d + 6], f_r.at[d + 6], yp(d)) for d in range(1, 8)]
    csum = lax.dot_general(r, onehot, NT, preferred_element_type=F32)
    cross_ref[...] = csum / jnp.maximum(counts[0:1, :], 1.0)
    for cp in zc:
        cp.wait_recv()
    cps = [put(cb.at[:, x, c], cb.at[:, x, c], f_s.at[d + 13], f_r.at[d + 13], xp(d)) for d in (1, 2, 3)]
    for cp in cps:
        cp.wait_recv()
    cp = put(cb.at[:, :, c], cb.at[:, :, c], f_s.at[17], f_r.at[17], sib)
    for q in yc:
        q.wait_recv()
    cp.wait_recv()
    rows = rb[...].reshape(128, 512)
    for zz in range(8):
        g = lax.dot_general(rows, cb[zz].reshape(128, 512), NT, preferred_element_type=F32)
        gt[:, :, zz * 128:(zz + 1) * 128] = (g * (1.0 / 512.0)).astype(BF16).reshape(8, 16, 128)
    cps = [put(gt.at[lax.rem(y + d, 8)], gr.at[y], f_s.at[d + 17], f_r.at[d + 17], yp(d)) for d in range(1, 8)]
    gr[y] = gt[y]
    for cp in cps:
        cp.wait_recv()
    for yy in range(8):
        for zz in range(8):
            o = (zz * 2 + yy // 4) * 512 + (yy % 4) * 128
            gram_ref[:, o:o + 128] = gr[yy, :, zz * 128:(zz + 1) * 128].astype(F32)

    for cp in sends:
        cp.wait_send()

    def drain(k, _):
        for s in streams:
            ring(k, s).wait_send()
        return 0

    lax.fori_loop(0, 7, drain, 0)


def on_device(resid_in, norm_gain, gate_weight, up_weight, down_weight, labels):
    vm = pl.BlockSpec(memory_space=pltpu.VMEM)
    hbm = pl.BlockSpec(memory_space=pltpu.HBM)
    dma = pltpu.SemaphoreType.DMA
    scratch = [
        pltpu.VMEM((4, 4, 2, 16, 512), BF16),
        pltpu.VMEM((512, 512), BF16),
        pltpu.VMEM((512, 896), BF16),
        pltpu.VMEM((512, 896), BF16),
        pltpu.VMEM((896, 512), BF16),
        pltpu.VMEM((512, 896), BF16),
        pltpu.VMEM((8, 128), F32),
        pltpu.VMEM((7, 8, 128), F32),
        pltpu.VMEM((2, 8, 128), F32),
        pltpu.VMEM((2, 2, 32, 896), F32),
        pltpu.VMEM((7, 2, 2, 32, 896), BF16),
        pltpu.VMEM((7, 2, 2, 32, 896), BF16),
        pltpu.VMEM((2, 2, 32, 896), F32),
        pltpu.VMEM((2, 2, 32, 896), BF16),
        pltpu.VMEM((2, 2, 32, 896), BF16),
        pltpu.VMEM((8, 2, 32, 896), BF16),
        pltpu.VMEM((4, 4, 2, 16, 512), F32),
        pltpu.VMEM((4, 4, 16, 512), BF16),
        pltpu.VMEM((4, 4, 16, 512), BF16),
        pltpu.VMEM((4, 4, 16, 512), F32),
        pltpu.VMEM((4, 4, 16, 512), BF16),
        pltpu.VMEM((3, 4, 16, 512), BF16),
        pltpu.VMEM((4, 16, 512), BF16),
        pltpu.VMEM((3, 16, 512), BF16),
        pltpu.VMEM((8, 4, 2, 16, 512), BF16),
        pltpu.VMEM((8, 16, 512), BF16),
        pltpu.VMEM((8, 16, 1024), BF16),
        pltpu.VMEM((8, 16, 1024), BF16),
        dma((3,)),
        dma((7,)), dma((7,)),
        dma((8,)), dma((8,)),
        dma((7, 2, 2)), dma((7, 2, 2)),
        dma((2, 2)), dma((2, 2)),
        dma((4, 2, 2)), dma((4, 2, 2)),
        dma((7,)), dma((7,)),
        dma((25,)), dma((25,)),
    ]
    return pl.pallas_call(
        kernel,
        out_shape=(jax.ShapeDtypeStruct((16, 8192), F32), jax.ShapeDtypeStruct((16, CLASSES), F32)),
        in_specs=[vm, vm, hbm, hbm, hbm, vm],
        out_specs=(vm, vm),
        scratch_shapes=scratch,
        compiler_params=pltpu.CompilerParams(
            collective_id=0, has_side_effects=True, vmem_limit_bytes=60 * 2**20),
    )(resid_in, norm_gain.reshape(1, -1), gate_weight, up_weight, down_weight, labels.reshape(1, -1))


def solution(mesh):
    return jax.shard_map(
        on_device,
        mesh=mesh,
        in_specs=(P("hid", "tok"), P("tok"), P("tok", "hid"), P("tok", "hid"), P("hid", "tok"), P()),
        out_specs=(P(("tok", "hid"), None), P(("tok", "hid"), None)),
        check_vma=False,
    )
```

time: 691 us -> 122 us (0.18)
  waiting for transfers between devices: 505 us -> 0 us
  blocking collectives: 155 us -> 0 us
  Pallas kernels: 0 us -> 119 us
  matrix products: 13.5 us -> 0 us
  between operations: 13.8 us -> 0.65 us
    reduce_scatter x2 -> x0, waiting for transfers between devices: 375 us -> none  [the longest x1 217 us: on_device(): lax.psum_scatter(jnp.dot(normed, both_weights, preferred_element_type=jnp...]
    all_gather x1 -> x0, waiting for transfers between devices: 130 us -> none  [on_device(): lax.all_gather(resid_cols, ('tok', 'hid'), axis=1, tiled=True)]
    pallas_call x0 -> x1, Pallas kernels: none -> 119 us  [on_device(): pl.pallas_call(kernel, out_shape=(jax.ShapeDtypeStruct((16, 8192), F32),...]
    all_gather x2 -> x0, blocking collectives: 104 us -> none  [the longest x1 57.8 us: on_device(): lax.all_gather(hidden, 'tok', axis=0, tiled=True)]
    psum x1 -> x0, blocking collectives: 50.9 us -> none  [on_device(): total_sq = lax.psum(local_sq, 'tok')]
    dot_general x4 -> x0, matrix products: 13.5 us -> none  [the longest x1 6.49 us: on_device(): lax.dot_general(resid_cols, lax.all_gather(resid_cols, ('tok', 'hid'), ax...]
  transfers between devices with their start and end apart: 3 -> 0, of which waited for: 3 -> 0; matrix products, arithmetic and copies ran while one was open for 0% -> 0% of each run, Pallas kernels for 0% -> 0%
where the time goes in v1:
time: 122 us
  Pallas kernels  119 us (98%)
  local copies, waits for them, and re-layouts  2.48 us (2%)
    pallas_call x1, Pallas kernels, on_device(): pl.pallas_call(kernel, out_shape=(jax.ShapeDtypeStruct((16, 8192), F32),...  119 us
    unnamed x4, local copies, waits for them, and re-layouts  2.48 us

profile of v1, /device:TPU:1, one launch (start us, length us, event | category | flops | bytes accessed | tf_op | source)
XLA Modules:
  0.0 121.9 jit_solution(6968132168195929768)
XLA Ops:
  0.6 118.8 %shard_map.77 = (f32[16,8192]{1,0:T(8,128)}, f32[16,64]{1,0:T(8,128)}) custom-call(bf16[16,512]{1,0:T(8,128)(2,1)} %x_ref.1, f32[1,512]{1,0:T(1,128)} %bitcast.2, bf16[512,896]{1,0:T(8,128)(2,1)} %wg_hbm.1, bf16[512,896]{1,0:T(8,128)(2,1)} %wu_hbm.1, bf16[896,512]{1,0:T(8,128)(2,1)} %wd_hbm.1, s32[1,512]{1,0:T(1,128)} %bitcast.3), custom_call_target="tpu_custom_call" | custom-call | tf_op jit(solution)/shard_map/pallas_call | solution.py:294
  119.4 0.0 copy-start
  119.4 1.9 %copy.10 = f32[16,8192]{1,0:T(8,128)} copy(f32[16,8192]{1,0:T(8,128)} %get-tuple-element.4) | data formatting | bytes 1048576
  121.3 0.0 copy-done
  121.3 0.6 copy.11
Async XLA Ops:
  119.4 1.9 %copy-start = (f32[16,64]{1,0:T(8,128)S(1)}, f32[16,64]{1,0:T(8,128)}, u32[]{:S(2)}) copy-start(f32[16,64]{1,0:T(8,128)} %get-tuple-element.5) | copy-start | bytes 12292

commit v2 on v1

v2 whole, which is shorter than its diff:
```python
import jax
import jax.numpy as jnp
from jax import lax
from jax.experimental import pallas as pl
from jax.experimental.pallas import tpu as pltpu
from jax.sharding import PartitionSpec as P

CLASSES = 64
EPS = 1e-05
F32 = jnp.float32
BF16 = jnp.bfloat16
MESH = pl.DeviceIdType.MESH
NT = (((1,), (1,)), ((), ()))


def kernel(x_ref, gain_ref, wg_hbm, wu_hbm, wd_hbm, lab_ref, gram_ref, cross_ref,
           xg, xn, wg, wu, wd, wdt, sqb, sqz, sqp, cown, csend, crecv, fin, ysend, yrecv,
           hb, ot, es, er, ea, ex, exr, ey, eyr, cb, rb, gt, gr,
           wsem, a_s, a_r, q_s, q_r, c_s, c_r, y_s, y_r, d_s, d_r, e_s, e_r, f_s, f_r):
    t = lax.axis_index("tok")
    h = lax.axis_index("hid")
    z, yh = t // 2, lax.rem(t, 2)
    yl, x, c = h // 8, lax.rem(h // 2, 4), lax.rem(h, 2)
    y = yh * 4 + yl

    def at(z=z, y=y, x=x, c=c):
        return {"tok": z * 2 + y // 4, "hid": (lax.rem(y, 4) * 4 + x) * 2 + c}

    def zp(d):
        return at(z=lax.rem(z + d, 8))

    def yp(d):
        return at(y=lax.rem(y + d, 8))

    def ylp(d):
        return at(y=yh * 4 + lax.rem(yl + d, 4))

    def xp(d):
        return at(x=lax.rem(x + d, 4))

    sib = at(c=1 - c)
    part = yp(4)

    loads = [pltpu.make_async_copy(a, b, wsem.at[i])
             for i, (a, b) in enumerate(((wg_hbm, wg), (wu_hbm, wu), (wd_hbm, wd)))]
    for cp in loads:
        cp.start()

    barrier = pltpu.get_barrier_semaphore()
    peers = [zp(d) for d in range(1, 8)] + [yp(d) for d in range(1, 8)]
    peers += [xp(d) for d in range(1, 4)] + [sib]
    for p in peers:
        pl.semaphore_signal(barrier, inc=1, device_id=p, device_id_type=MESH)
    xg[yl, x, c] = x_ref[...]
    pl.semaphore_wait(barrier, len(peers))

    sends = []

    def put(src, dst, sem, i, dev):
        cp = pltpu.make_async_remote_copy(src_ref=src, dst_ref=dst, send_sem=sem[0].at[i], recv_sem=sem[1].at[i],
                                          device_id=dev, device_id_type=MESH)
        cp.start()
        sends.append(cp)
        return cp

    sa = (a_s, a_r)
    ycp = [put(xg.at[yl, x, c], xg.at[yl, x, c], sa, d - 1, ylp(d)) for d in (1, 2, 3)]
    xcp = [[put(xg.at[yl, x, c], xg.at[yl, x, c], sa, d + 2, xp(d)) for d in (1, 2, 3)]]
    loads[2].wait()
    wdt[...] = wd[...].T
    for d in (1, 2, 3):
        ycp[d - 1].wait_recv()
        b = lax.rem(yl + 4 - d, 4)
        xcp.append([put(xg.at[b, x, c], xg.at[b, x, c], sa, 3 * d + e + 2, xp(e)) for e in (1, 2, 3)])
    scp = []
    for d in range(4):
        for cp in xcp[d]:
            cp.wait_recv()
        b = lax.rem(yl + 4 - d, 4)
        scp.append(put(xg.at[b, :, c], xg.at[b, :, c], sa, 15 + d, sib))
    loads[0].wait()
    loads[1].wait()
    for cp in scp:
        cp.wait_recv()

    xa = xg[...].reshape(512, 512)
    xf = xa.astype(F32)
    xn[...] = (xf * gain_ref[...]).astype(BF16)

    def own(r):
        q = lax.rem(z + r, 8)
        rows = xn[pl.ds(pl.multiple_of(q * 64, 64), 64), :]
        cown[r, :, :, :896] = jnp.dot(rows, wg[...], preferred_element_type=F32).reshape(4, 16, 896)
        cown[r, :, :, 896:] = jnp.dot(rows, wu[...], preferred_element_type=F32).reshape(4, 16, 896)

    right, left = zp(1), zp(7)
    sc = (c_s, c_r)
    ring = {}

    def hop(k, way, s, add):
        r = 4 - k if way == 0 else 4 + k
        v = cown[r, s]
        if add:
            ring[k - 1, way, s].wait_recv()
            v = v + crecv[k - 1, way, s].astype(F32)
        csend[k, way, s] = v.astype(BF16)
        ring[k, way, s] = put(csend.at[k, way, s], crecv.at[k, way, s], sc, (k, way, s), right if way == 0 else left)

    own(4)
    for i in (0, 1):
        hop(0, 0, i, False)
        hop(0, 1, 2 + i, False)
    own(3)
    own(5)
    for i in (0, 1):
        hop(1, 0, 2 + i, False)
        hop(1, 1, i, False)

    x2 = xf * xf
    hi = x2.astype(BF16)
    lo = (x2 - hi.astype(F32)).astype(BF16)
    ones = jnp.ones((8, 512), BF16)
    sq = (lax.dot_general(ones, hi, NT, preferred_element_type=F32)
          + lax.dot_general(ones, lo, NT, preferred_element_type=F32))
    sqb[...] = jnp.zeros_like(sqb)
    for k in range(4):
        sqb[k:k + 1, :] = sq[0:1, k * 128:(k + 1) * 128]
    sqs = (q_s, q_r)
    qcps = [put(sqb, sqz.at[d - 1], sqs, d - 1, zp(d)) for d in range(1, 8)]

    for i in (0, 1):
        hop(1, 0, i, True)
        hop(1, 1, 2 + i, True)
    order = [(0, 2), (1, 0), (0, 3), (1, 1), (0, 0), (1, 2), (0, 1), (1, 3)]
    own(2)
    own(6)
    for way, s in order:
        hop(2, way, s, True)
    own(1)
    own(7)
    for way, s in order:
        hop(3, way, s, True)
    own(0)

    for cp in qcps:
        cp.wait_recv()
    tot = sqb[...]
    for d in range(7):
        tot = tot + sqz[d]
    sqp[0] = tot
    qy = put(sqp.at[0], sqp.at[1], sqs, 7, part)
    sel = (lax.broadcasted_iota(jnp.int32, (16, 512), 1)
           == lax.broadcasted_iota(jnp.int32, (16, 512), 0) + h * 16).astype(BF16)
    xcols = lax.dot_general(sel, xa, NT, preferred_element_type=F32)
    onehot = (lax.broadcasted_iota(jnp.int32, (CLASSES, 512), 0) == lab_ref[...]).astype(BF16)
    counts = lax.dot_general(ones, onehot, NT, preferred_element_type=F32)

    srow = (2, 0, 3, 1)
    sy = (y_s, y_r)
    ycps = {}
    for s in srow:
        ring[3, 0, s].wait_recv()
        ring[3, 1, s].wait_recv()
        v = cown[0, s] + crecv[3, 0, s].astype(F32) + crecv[3, 1, s].astype(F32)
        fin[s] = v
        ysend[s] = v.astype(BF16)
        ycps[s] = put(ysend.at[s], yrecv.at[s], sy, s, part)
    qy.wait_recv()
    tot = sqp[0] + sqp[1]
    tix = (lax.broadcasted_iota(jnp.int32, (64, 128), 0) + z * 64
           - lax.broadcasted_iota(jnp.int32, (64, 128), 1))
    pick = jnp.zeros((64, 128), F32)
    for k in range(4):
        pick = pick + jnp.where(tix == k * 128, tot[k:k + 1, :], 0.0)
    scale = lax.rsqrt(jnp.sum(pick, axis=1, keepdims=True) / 8192.0 + EPS)

    sd = (d_s, d_r)

    def dput(k, way, s):
        q = lax.rem(z + 8 - k, 8) if way == 0 else lax.rem(z + k, 8)
        return put(hb.at[q, s], hb.at[q, s], sd, (k, way, s), right if way == 0 else left)

    live = {}
    for s in srow:
        ycps[s].wait_recv()
        v = (fin[s] + yrecv[s].astype(F32)) * scale[s * 16:(s + 1) * 16, :]
        gate, up = v[:, :896], v[:, 896:]
        hb[z, s] = (gate / (1.0 + jnp.exp(-gate)) * up).astype(BF16)
        for way in (0, 1):
            live[0, way, s] = dput(0, way, s)
    for k in (1, 2, 3):
        for s in srow:
            for way in (0, 1):
                live[k - 1, way, s].wait_recv()
                if k < 3 or way == s // 2:
                    live[k, way, s] = dput(k, way, s)
    for s in srow:
        live[3, s // 2, s].wait_recv()

    se = (e_s, e_r)
    hall = hb[...].reshape(512, 896)
    eo = (2, 1, 3, 0)
    scp = {}
    for d in eo:
        b = lax.rem(yl + d, 4)
        w = wdt[pl.ds(pl.multiple_of(b * 128, 128), 128), :]
        ot[d] = lax.dot_general(w, hall, NT, preferred_element_type=F32).reshape(4, 2, 16, 512)
        es[d] = ot[d, :, 1 - c].astype(BF16)
        scp[d] = put(es.at[d], er.at[d], se, d, sib)
    xcp = {}
    for d in eo:
        scp[d].wait_recv()
        v = ot[d, :, c] + er[d].astype(F32)
        ea[d] = v
        ex[d] = v.astype(BF16)
        xcp[d] = [put(ex.at[d, lax.rem(x + e, 4)], exr.at[d, e - 1], se, 3 + 3 * d + e, xp(e)) for e in (2, 1, 3)]
    ycp = []
    for d in eo:
        for cp in xcp[d]:
            cp.wait_recv()
        v = ea[d, x]
        for e in range(3):
            v = v + exr[d, e].astype(F32)
        if d:
            ey[d - 1] = v.astype(BF16)
            ycp.append(put(ey.at[d - 1], eyr.at[d - 1], se, 15 + d, ylp(d)))
    for cp in ycp:
        cp.wait_recv()
    for d in range(3):
        v = v + eyr[d].astype(F32)
    r = (xcols + v).astype(BF16)

    sf = (f_s, f_r)
    cb[z, x, c] = r
    rb[y] = r
    mine = cb.at[z, x, c]
    zcp = {d: put(mine, mine, sf, d, zp(d)) for d in (4, 3, 5, 2, 6, 1, 7)}
    xcp = {0: [put(mine, mine, sf, 7 + e, xp(e)) for e in (2, 1, 3)]}
    ycp = [put(mine, rb.at[y], sf, 10 + d, yp(d)) for d in (4, 3, 5, 2, 6, 1, 7)]
    csum = lax.dot_general(r, onehot, NT, preferred_element_type=F32)
    cross_ref[...] = csum / jnp.maximum(counts[0:1, :], 1.0)
    fo = (0, 1, 7, 2, 6, 3, 5, 4)
    for d in fo[1:]:
        zcp[d].wait_recv()
        blk = cb.at[lax.rem(z + 8 - d, 8), x, c]
        xcp[d] = [put(blk, blk, sf, 17 + 3 * d - 3 + e, xp(e)) for e in (2, 1, 3)]
    scp = {}
    for d in fo:
        for cp in xcp[d]:
            cp.wait_recv()
        blk = cb.at[lax.rem(z + 8 - d, 8), :, c]
        scp[d] = put(blk, blk, sf, 39 + d, sib)
    for cp in ycp:
        cp.wait_recv()
    rows = rb[...].reshape(128, 512)
    gcp = []
    for i, d in enumerate(fo):
        scp[d].wait_recv()
        g = lax.dot_general(rows, cb[lax.rem(z + 8 - d, 8)].reshape(128, 512), NT, preferred_element_type=F32)
        gt[i // 4, :, :, i % 4 * 128:(i % 4 + 1) * 128] = (g * (1.0 / 512.0)).astype(BF16).reshape(8, 16, 128)
        if i % 4 == 3:
            p = i // 4
            gcp += [put(gt.at[p, lax.rem(y + e, 8)], gr.at[p, y], sf, 46 + 7 * p + e, yp(e))
                    for e in (4, 3, 5, 2, 6, 1, 7)]
            gr[p, y] = gt[p, y]
    for cp in gcp:
        cp.wait_recv()
    for i, d in enumerate(fo):
        q = lax.rem(z + 8 - d, 8)
        for yy in range(8):
            o = pl.multiple_of((q * 2 + yy // 4) * 512 + yy % 4 * 128, 128)
            gram_ref[:, pl.ds(o, 128)] = gr[i // 4, yy, :, i % 4 * 128:(i % 4 + 1) * 128].astype(F32)

    for cp in sends:
        cp.wait_send()


def on_device(resid_in, norm_gain, gate_weight, up_weight, down_weight, labels):
    vm = pl.BlockSpec(memory_space=pltpu.VMEM)
    hbm = pl.BlockSpec(memory_space=pltpu.HBM)
    dma = pltpu.SemaphoreType.DMA
    scratch = [
        pltpu.VMEM((4, 4, 2, 16, 512), BF16),
        pltpu.VMEM((512, 512), BF16),
        pltpu.VMEM((512, 896), BF16),
        pltpu.VMEM((512, 896), BF16),
        pltpu.VMEM((896, 512), BF16),
        pltpu.VMEM((512, 896), BF16),
        pltpu.VMEM((8, 128), F32),
        pltpu.VMEM((7, 8, 128), F32),
        pltpu.VMEM((2, 8, 128), F32),
        pltpu.VMEM((8, 4, 16, 1792), F32),
        pltpu.VMEM((4, 2, 4, 16, 1792), BF16),
        pltpu.VMEM((4, 2, 4, 16, 1792), BF16),
        pltpu.VMEM((4, 16, 1792), F32),
        pltpu.VMEM((4, 16, 1792), BF16),
        pltpu.VMEM((4, 16, 1792), BF16),
        pltpu.VMEM((8, 4, 16, 896), BF16),
        pltpu.VMEM((4, 4, 2, 16, 512), F32),
        pltpu.VMEM((4, 4, 16, 512), BF16),
        pltpu.VMEM((4, 4, 16, 512), BF16),
        pltpu.VMEM((4, 4, 16, 512), F32),
        pltpu.VMEM((4, 4, 16, 512), BF16),
        pltpu.VMEM((4, 3, 16, 512), BF16),
        pltpu.VMEM((3, 16, 512), BF16),
        pltpu.VMEM((3, 16, 512), BF16),
        pltpu.VMEM((8, 4, 2, 16, 512), BF16),
        pltpu.VMEM((8, 16, 512), BF16),
        pltpu.VMEM((2, 8, 16, 512), BF16),
        pltpu.VMEM((2, 8, 16, 512), BF16),
        dma((3,)),
        dma((19,)), dma((19,)),
        dma((8,)), dma((8,)),
        dma((4, 2, 4)), dma((4, 2, 4)),
        dma((4,)), dma((4,)),
        dma((4, 2, 4)), dma((4, 2, 4)),
        dma((19,)), dma((19,)),
        dma((61,)), dma((61,)),
    ]
    return pl.pallas_call(
        kernel,
        out_shape=(jax.ShapeDtypeStruct((16, 8192), F32), jax.ShapeDtypeStruct((16, CLASSES), F32)),
        in_specs=[vm, vm, hbm, hbm, hbm, vm],
        out_specs=(vm, vm),
        scratch_shapes=scratch,
        compiler_params=pltpu.CompilerParams(
            collective_id=0, has_side_effects=True, vmem_limit_bytes=60 * 2**20),
    )(resid_in, norm_gain.reshape(1, -1), gate_weight, up_weight, down_weight, labels.reshape(1, -1))


def solution(mesh):
    return jax.shard_map(
        on_device,
        mesh=mesh,
        in_specs=(P("hid", "tok"), P("tok"), P("tok", "hid"), P("tok", "hid"), P("hid", "tok"), P()),
        out_specs=(P(("tok", "hid"), None), P(("tok", "hid"), None)),
        check_vma=False,
    )
```

time: 122 us -> 105 us (0.86)
  Pallas kernels: 119 us -> 101 us
    pallas_call x1, Pallas kernels: 119 us -> 101 us  [on_device(): pl.pallas_call(kernel, out_shape=(jax.ShapeDtypeStruct((16, 8192), F32),...]
where the time goes in v2:
time: 105 us; the launch traced here: 104 us
  Pallas kernels  101 us (96%)
  local copies, waits for them, and re-layouts  2.48 us (2%)
    pallas_call x1, Pallas kernels, on_device(): pl.pallas_call(kernel, out_shape=(jax.ShapeDtypeStruct((16, 8192), F32),...  101 us
    unnamed x4, local copies, waits for them, and re-layouts  2.48 us

profile of v2, /device:TPU:1, one launch (start us, length us, event | category | flops | bytes accessed | tf_op | source)
XLA Modules:
  0.0 104.4 jit_solution(5697955979457646282)
XLA Ops:
  0.6 101.3 %shard_map.77 = (f32[16,8192]{1,0:T(8,128)}, f32[16,64]{1,0:T(8,128)}) custom-call(bf16[16,512]{1,0:T(8,128)(2,1)} %x_ref.1, f32[1,512]{1,0:T(1,128)} %bitcast.2, bf16[512,896]{1,0:T(8,128)(2,1)} %wg_hbm.1, bf16[512,896]{1,0:T(8,128)(2,1)} %wu_hbm.1, bf16[896,512]{1,0:T(8,128)(2,1)} %wd_hbm.1, s32[1,512]{1,0:T(1,128)} %bitcast.3), custom_call_target="tpu_custom_call" | custom-call | tf_op jit(solution)/shard_map/pallas_call | solution.py:320
  101.9 0.0 copy-start
  101.9 1.9 %copy.10 = f32[16,8192]{1,0:T(8,128)} copy(f32[16,8192]{1,0:T(8,128)} %get-tuple-element.4) | data formatting | bytes 1048576
  103.8 0.0 copy-done
  103.8 0.6 copy.11
Async XLA Ops:
  101.9 1.9 %copy-start = (f32[16,64]{1,0:T(8,128)S(1)}, f32[16,64]{1,0:T(8,128)}, u32[]{:S(2)}) copy-start(f32[16,64]{1,0:T(8,128)} %get-tuple-element.5) | copy-start | bytes 12292

commit v3 on v2

--- a/solution.py
+++ b/solution.py
@@ -14,8 +14,8 @@
 
 
 def kernel(x_ref, gain_ref, wg_hbm, wu_hbm, wd_hbm, lab_ref, gram_ref, cross_ref,
-           xg, xn, wg, wu, wd, wdt, sqb, sqz, sqp, cown, csend, crecv, fin, ysend, yrecv,
-           hb, ot, es, er, ea, ex, exr, ey, eyr, cb, rb, gt, gr,
+           xg, xn, wg, wu, wd, wdt, sqb, sqz, sqp, cown0, cown1, csend0, csend1, crecv0, crecv1,
+           fin0, fin1, ysend0, ysend1, yrecv0, yrecv1, hb0, hb1, ot, es, er, ea, ex, exr, ey, eyr, cb, rb, gt, gr,
            wsem, a_s, a_r, q_s, q_r, c_s, c_r, y_s, y_r, d_s, d_r, e_s, e_r, f_s, f_r):
     t = lax.axis_index("tok")
     h = lax.axis_index("hid")
@@ -47,8 +47,8 @@
         cp.start()
 
     barrier = pltpu.get_barrier_semaphore()
-    peers = [zp(d) for d in range(1, 8)] + [yp(d) for d in range(1, 8)]
-    peers += [xp(d) for d in range(1, 4)] + [sib]
+    peers = [yp(d) for d in range(1, 8)] + [xp(d) for d in range(1, 4)] + [sib]
+    peers += [zp(d) for d in range(1, 8)]
     for p in peers:
         pl.semaphore_signal(barrier, inc=1, device_id=p, device_id_type=MESH)
     xg[yl, x, c] = x_ref[...]
@@ -64,14 +64,14 @@
         return cp
 
     sa = (a_s, a_r)
-    ycp = [put(xg.at[yl, x, c], xg.at[yl, x, c], sa, d - 1, ylp(d)) for d in (1, 2, 3)]
-    xcp = [[put(xg.at[yl, x, c], xg.at[yl, x, c], sa, d + 2, xp(d)) for d in (1, 2, 3)]]
+    ycp = {d: put(xg.at[yl, x, c], xg.at[yl, x, c], sa, d - 1, ylp(d)) for d in (2, 3, 1)}
+    xcp = [[put(xg.at[yl, x, c], xg.at[yl, x, c], sa, d + 2, xp(d)) for d in (2, 1, 3)]]
     loads[2].wait()
     wdt[...] = wd[...].T
     for d in (1, 2, 3):
-        ycp[d - 1].wait_recv()
+        ycp[d].wait_recv()
         b = lax.rem(yl + 4 - d, 4)
-        xcp.append([put(xg.at[b, x, c], xg.at[b, x, c], sa, 3 * d + e + 2, xp(e)) for e in (1, 2, 3)])
+        xcp.append([put(xg.at[b, x, c], xg.at[b, x, c], sa, 3 * d + e + 2, xp(e)) for e in (2, 1, 3)])
     scp = []
     for d in range(4):
         for cp in xcp[d]:
@@ -87,34 +87,54 @@
     xf = xa.astype(F32)
     xn[...] = (xf * gain_ref[...]).astype(BF16)
 
+    cown, csend, crecv = (cown0, cown1), (csend0, csend1), (crecv0, crecv1)
+    fin, ysend, yrecv, hb = (fin0, fin1), (ysend0, ysend1), (yrecv0, yrecv1), (hb0, hb1)
+    width = (512, 384)
+
     def own(r):
         q = lax.rem(z + r, 8)
         rows = xn[pl.ds(pl.multiple_of(q * 64, 64), 64), :]
-        cown[r, :, :, :896] = jnp.dot(rows, wg[...], preferred_element_type=F32).reshape(4, 16, 896)
-        cown[r, :, :, 896:] = jnp.dot(rows, wu[...], preferred_element_type=F32).reshape(4, 16, 896)
+        for b in (0, 1):
+            n, lo = width[b], 512 * b
+            for i, w in ((0, wg), (1, wu)):
+                v = jnp.dot(rows, w[:, lo:lo + n], preferred_element_type=F32)
+                cown[b][r, :, :, i * n:(i + 1) * n] = v.reshape(2, 32, n)
 
     right, left = zp(1), zp(7)
     sc = (c_s, c_r)
     ring = {}
 
-    def hop(k, way, s, add):
-        r = 4 - k if way == 0 else 4 + k
-        v = cown[r, s]
+    def hop(b, k, way, s, add):
+        v = cown[b][4 - k if way == 0 else 4 + k, s]
         if add:
-            ring[k - 1, way, s].wait_recv()
-            v = v + crecv[k - 1, way, s].astype(F32)
-        csend[k, way, s] = v.astype(BF16)
-        ring[k, way, s] = put(csend.at[k, way, s], crecv.at[k, way, s], sc, (k, way, s), right if way == 0 else left)
+            ring[b, k - 1, way, s].wait_recv()
+            v = v + crecv[b][k - 1, way, s].astype(F32)
+        csend[b][k, way, s] = v.astype(BF16)
+        ring[b, k, way, s] = put(csend[b].at[k, way, s], crecv[b].at[k, way, s], sc, (b, k, way, s),
+                                 right if way == 0 else left)
+
+    def first(b):
+        hop(b, 0, 0, 0, False)
+        hop(b, 0, 1, 1, False)
+
+    def second(b):
+        hop(b, 1, 0, 1, False)
+        hop(b, 1, 1, 0, False)
+
+    def third(b):
+        hop(b, 1, 0, 0, True)
+        hop(b, 1, 1, 1, True)
+
+    def later(b, k):
+        for way, s in ((0, 1), (1, 0), (0, 0), (1, 1)):
+            hop(b, k, way, s, True)
 
     own(4)
-    for i in (0, 1):
-        hop(0, 0, i, False)
-        hop(0, 1, 2 + i, False)
+    first(0)
     own(3)
     own(5)
-    for i in (0, 1):
-        hop(1, 0, 2 + i, False)
-        hop(1, 1, i, False)
+    second(0)
+    first(1)
 
     x2 = xf * xf
     hi = x2.astype(BF16)
@@ -126,22 +146,40 @@
     for k in range(4):
         sqb[k:k + 1, :] = sq[0:1, k * 128:(k + 1) * 128]
     sqs = (q_s, q_r)
-    qcps = [put(sqb, sqz.at[d - 1], sqs, d - 1, zp(d)) for d in range(1, 8)]
-
-    for i in (0, 1):
-        hop(1, 0, i, True)
-        hop(1, 1, 2 + i, True)
-    order = [(0, 2), (1, 0), (0, 3), (1, 1), (0, 0), (1, 2), (0, 1), (1, 3)]
+    third(0)
+    second(1)
     own(2)
     own(6)
-    for way, s in order:
-        hop(2, way, s, True)
+    later(0, 2)
+    third(1)
+    qcps = [put(sqb, sqz.at[d - 1], sqs, d - 1, zp(d)) for d in range(1, 8)]
     own(1)
     own(7)
-    for way, s in order:
-        hop(3, way, s, True)
+    later(0, 3)
+    later(1, 2)
     own(0)
 
+    sel = (lax.broadcasted_iota(jnp.int32, (16, 512), 1)
+           == lax.broadcasted_iota(jnp.int32, (16, 512), 0) + h * 16).astype(BF16)
+    xcols = lax.dot_general(sel, xa, NT, preferred_element_type=F32)
+    onehot = (lax.broadcasted_iota(jnp.int32, (CLASSES, 512), 0) == lab_ref[...]).astype(BF16)
+    counts = lax.dot_general(ones, onehot, NT, preferred_element_type=F32)
+
+    sy = (y_s, y_r)
+
+    def swap(b):
+        cps = []
+        for s in (0, 1):
+            for way in (0, 1):
+                ring[b, 3, way, s].wait_recv()
+            v = cown[b][0, s] + crecv[b][3, 0, s].astype(F32) + crecv[b][3, 1, s].astype(F32)
+            fin[b][s] = v
+            ysend[b][s] = v.astype(BF16)
+            cps.append(put(ysend[b].at[s], yrecv[b].at[s], sy, (b, s), part))
+        return cps
+
+    ycps = [swap(0)]
+    later(1, 3)
     for cp in qcps:
         cp.wait_recv()
     tot = sqb[...]
@@ -149,22 +187,7 @@
         tot = tot + sqz[d]
     sqp[0] = tot
     qy = put(sqp.at[0], sqp.at[1], sqs, 7, part)
-    sel = (lax.broadcasted_iota(jnp.int32, (16, 512), 1)
-           == lax.broadcasted_iota(jnp.int32, (16, 512), 0) + h * 16).astype(BF16)
-    xcols = lax.dot_general(sel, xa, NT, preferred_element_type=F32)
-    onehot = (lax.broadcasted_iota(jnp.int32, (CLASSES, 512), 0) == lab_ref[...]).astype(BF16)
-    counts = lax.dot_general(ones, onehot, NT, preferred_element_type=F32)
-
-    srow = (2, 0, 3, 1)
-    sy = (y_s, y_r)
-    ycps = {}
-    for s in srow:
-        ring[3, 0, s].wait_recv()
-        ring[3, 1, s].wait_recv()
-        v = cown[0, s] + crecv[3, 0, s].astype(F32) + crecv[3, 1, s].astype(F32)
-        fin[s] = v
-        ysend[s] = v.astype(BF16)
-        ycps[s] = put(ysend.at[s], yrecv.at[s], sy, s, part)
+    ycps.append(swap(1))
     qy.wait_recv()
     tot = sqp[0] + sqp[1]
     tix = (lax.broadcasted_iota(jnp.int32, (64, 128), 0) + z * 64
@@ -175,36 +198,58 @@
     scale = lax.rsqrt(jnp.sum(pick, axis=1, keepdims=True) / 8192.0 + EPS)
 
     sd = (d_s, d_r)
-
-    def dput(k, way, s):
-        q = lax.rem(z + 8 - k, 8) if way == 0 else lax.rem(z + k, 8)
-        return put(hb.at[q, s], hb.at[q, s], sd, (k, way, s), right if way == 0 else left)
-
     live = {}
-    for s in srow:
-        ycps[s].wait_recv()
-        v = (fin[s] + yrecv[s].astype(F32)) * scale[s * 16:(s + 1) * 16, :]
-        gate, up = v[:, :896], v[:, 896:]
-        hb[z, s] = (gate / (1.0 + jnp.exp(-gate)) * up).astype(BF16)
-        for way in (0, 1):
-            live[0, way, s] = dput(0, way, s)
-    for k in (1, 2, 3):
-        for s in srow:
-            for way in (0, 1):
-                live[k - 1, way, s].wait_recv()
-                if k < 3 or way == s // 2:
-                    live[k, way, s] = dput(k, way, s)
-    for s in srow:
-        live[3, s // 2, s].wait_recv()
+
+    def dput(b, r, s, j, d):
+        blk = hb[b].at[lax.rem(z + r, 8), s]
+        live[b, j, s] = put(blk, blk, sd, (b, j, s), zp(d))
+
+    def hidden(b):
+        n = width[b]
+        for s in (0, 1):
+            ycps[b][s].wait_recv()
+            v = (fin[b][s] + yrecv[b][s].astype(F32)) * scale[s * 32:(s + 1) * 32, :]
+            gate, up = v[:, :n], v[:, n:]
+            hb[b][z, s] = (gate / (1.0 + jnp.exp(-gate)) * up).astype(BF16)
+            for j, d in enumerate((2, 6, 1, 7)):
+                dput(b, 0, s, j, d)
+
+    def onward(b):
+        for s in (0, 1):
+            live[b, 0, s].wait_recv()
+            if s == 0:
+                dput(b, 6, s, 6, 2)
+            dput(b, 6, s, 4, 1)
+            live[b, 1, s].wait_recv()
+            if s == 1:
+                dput(b, 2, s, 7, 6)
+            dput(b, 2, s, 5, 7)
+
+    def arrived(b):
+        for s in (0, 1):
+            for j in (2, 3, 4, 5, 6 + s):
+                live[b, j, s].wait_recv()
+
+    eo = (2, 1, 3, 0)
+
+    def down(b, d):
+        rows = wdt[pl.ds(pl.multiple_of(lax.rem(yl + d, 4) * 128, 128), 128), 512 * b:512 * b + width[b]]
+        v = lax.dot_general(rows, hb[b][...].reshape(512, width[b]), NT, preferred_element_type=F32)
+        return v.reshape(4, 2, 16, 512)
+
+    hidden(0)
+    onward(0)
+    hidden(1)
+    arrived(0)
+    onward(1)
+    for d in eo:
+        ot[d] = down(0, d)
+    arrived(1)
 
     se = (e_s, e_r)
-    hall = hb[...].reshape(512, 896)
-    eo = (2, 1, 3, 0)
     scp = {}
     for d in eo:
-        b = lax.rem(yl + d, 4)
-        w = wdt[pl.ds(pl.multiple_of(b * 128, 128), 128), :]
-        ot[d] = lax.dot_general(w, hall, NT, preferred_element_type=F32).reshape(4, 2, 16, 512)
+        ot[d] = ot[d] + down(1, d)
         es[d] = ot[d, :, 1 - c].astype(BF16)
         scp[d] = put(es.at[d], er.at[d], se, d, sib)
     xcp = {}
@@ -289,13 +334,20 @@
         pltpu.VMEM((8, 128), F32),
         pltpu.VMEM((7, 8, 128), F32),
         pltpu.VMEM((2, 8, 128), F32),
-        pltpu.VMEM((8, 4, 16, 1792), F32),
-        pltpu.VMEM((4, 2, 4, 16, 1792), BF16),
-        pltpu.VMEM((4, 2, 4, 16, 1792), BF16),
-        pltpu.VMEM((4, 16, 1792), F32),
-        pltpu.VMEM((4, 16, 1792), BF16),
-        pltpu.VMEM((4, 16, 1792), BF16),
-        pltpu.VMEM((8, 4, 16, 896), BF16),
+        pltpu.VMEM((8, 2, 32, 1024), F32),
+        pltpu.VMEM((8, 2, 32, 768), F32),
+        pltpu.VMEM((4, 2, 2, 32, 1024), BF16),
+        pltpu.VMEM((4, 2, 2, 32, 768), BF16),
+        pltpu.VMEM((4, 2, 2, 32, 1024), BF16),
+        pltpu.VMEM((4, 2, 2, 32, 768), BF16),
+        pltpu.VMEM((2, 32, 1024), F32),
+        pltpu.VMEM((2, 32, 768), F32),
+        pltpu.VMEM((2, 32, 1024), BF16),
+        pltpu.VMEM((2, 32, 768), BF16),
+        pltpu.VMEM((2, 32, 1024), BF16),
+        pltpu.VMEM((2, 32, 768), BF16),
+        pltpu.VMEM((8, 2, 32, 512), BF16),
+        pltpu.VMEM((8, 2, 32, 384), BF16),
         pltpu.VMEM((4, 4, 2, 16, 512), F32),
         pltpu.VMEM((4, 4, 16, 512), BF16),
         pltpu.VMEM((4, 4, 16, 512), BF16),
@@ -311,9 +363,9 @@
         dma((3,)),
         dma((19,)), dma((19,)),
         dma((8,)), dma((8,)),
-        dma((4, 2, 4)), dma((4, 2, 4)),
-        dma((4,)), dma((4,)),
-        dma((4, 2, 4)), dma((4, 2, 4)),
+        dma((2, 4, 2, 2)), dma((2, 4, 2, 2)),
+        dma((2, 2)), dma((2, 2)),
+        dma((2, 8, 2)), dma((2, 8, 2)),
         dma((19,)), dma((19,)),
         dma((61,)), dma((61,)),
     ]

time: 105 us -> 103 us (0.981)
  Pallas kernels: 101 us -> 99.5 us
    pallas_call x1, Pallas kernels: 101 us -> 99.5 us  [on_device(): pl.pallas_call(kernel, out_shape=(jax.ShapeDtypeStruct((16, 8192), F32),...]
where the time goes in v3:
time: 103 us
  Pallas kernels  99.5 us (97%)
  local copies, waits for them, and re-layouts  2.48 us (2%)
    pallas_call x1, Pallas kernels, on_device(): pl.pallas_call(kernel, out_shape=(jax.ShapeDtypeStruct((16, 8192), F32),...  99.5 us
    unnamed x4, local copies, waits for them, and re-layouts  2.48 us

profile of v3, /device:TPU:1, one launch (start us, length us, event | category | flops | bytes accessed | tf_op | source)
XLA Modules:
  0.0 102.6 jit_solution(9969314039602837238)
XLA Ops:
  0.6 99.5 %shard_map.77 = (f32[16,8192]{1,0:T(8,128)}, f32[16,64]{1,0:T(8,128)}) custom-call(bf16[16,512]{1,0:T(8,128)(2,1)} %x_ref.1, f32[1,512]{1,0:T(1,128)} %bitcast.2, bf16[512,896]{1,0:T(8,128)(2,1)} %wg_hbm.1, bf16[512,896]{1,0:T(8,128)(2,1)} %wu_hbm.1, bf16[896,512]{1,0:T(8,128)(2,1)} %wd_hbm.1, s32[1,512]{1,0:T(1,128)} %bitcast.3), custom_call_target="tpu_custom_call" | custom-call | tf_op jit(solution)/shard_map/pallas_call | solution.py:372
  100.2 0.0 copy-start
  100.2 1.9 %copy.10 = f32[16,8192]{1,0:T(8,128)} copy(f32[16,8192]{1,0:T(8,128)} %get-tuple-element.4) | data formatting | bytes 1048576
  102.0 0.0 copy-done
  102.0 0.6 copy.11
Async XLA Ops:
  100.2 1.9 %copy-start = (f32[16,64]{1,0:T(8,128)S(1)}, f32[16,64]{1,0:T(8,128)}, u32[]{:S(2)}) copy-start(f32[16,64]{1,0:T(8,128)} %get-tuple-element.5) | copy-start | bytes 12292

commit v4 on v3

--- a/solution.py
+++ b/solution.py
@@ -11,9 +11,10 @@
 BF16 = jnp.bfloat16
 MESH = pl.DeviceIdType.MESH
 NT = (((1,), (1,)), ((), ()))
-
-
-def kernel(x_ref, gain_ref, wg_hbm, wu_hbm, wd_hbm, lab_ref, gram_ref, cross_ref,
+ARRIVAL = (0, 1, 7, 2, 6, 3, 5, 4)
+
+
+def kernel(x_ref, gain_ref, wg_hbm, wu_hbm, wd_hbm, lab_ref, out_ref, cross_ref,
            xg, xn, wg, wu, wd, wdt, sqb, sqz, sqp, cown0, cown1, csend0, csend1, crecv0, crecv1,
            fin0, fin1, ysend0, ysend1, yrecv0, yrecv1, hb0, hb1, ot, es, er, ea, ex, exr, ey, eyr, cb, rb, gt, gr,
            wsem, a_s, a_r, q_s, q_r, c_s, c_r, y_s, y_r, d_s, d_r, e_s, e_r, f_s, f_r):
@@ -89,13 +90,13 @@
 
     cown, csend, crecv = (cown0, cown1), (csend0, csend1), (crecv0, crecv1)
     fin, ysend, yrecv, hb = (fin0, fin1), (ysend0, ysend1), (yrecv0, yrecv1), (hb0, hb1)
-    width = (512, 384)
+    width = (384, 512)
 
     def own(r):
         q = lax.rem(z + r, 8)
         rows = xn[pl.ds(pl.multiple_of(q * 64, 64), 64), :]
         for b in (0, 1):
-            n, lo = width[b], 512 * b
+            n, lo = width[b], width[0] * b
             for i, w in ((0, wg), (1, wu)):
                 v = jnp.dot(rows, w[:, lo:lo + n], preferred_element_type=F32)
                 cown[b][r, :, :, i * n:(i + 1) * n] = v.reshape(2, 32, n)
@@ -233,7 +234,7 @@
     eo = (2, 1, 3, 0)
 
     def down(b, d):
-        rows = wdt[pl.ds(pl.multiple_of(lax.rem(yl + d, 4) * 128, 128), 128), 512 * b:512 * b + width[b]]
+        rows = wdt[pl.ds(pl.multiple_of(lax.rem(yl + d, 4) * 128, 128), 128), width[0] * b:width[0] * b + width[b]]
         v = lax.dot_general(rows, hb[b][...].reshape(512, width[b]), NT, preferred_element_type=F32)
         return v.reshape(4, 2, 16, 512)
 
@@ -284,7 +285,7 @@
     ycp = [put(mine, rb.at[y], sf, 10 + d, yp(d)) for d in (4, 3, 5, 2, 6, 1, 7)]
     csum = lax.dot_general(r, onehot, NT, preferred_element_type=F32)
     cross_ref[...] = csum / jnp.maximum(counts[0:1, :], 1.0)
-    fo = (0, 1, 7, 2, 6, 3, 5, 4)
+    fo = ARRIVAL
     for d in fo[1:]:
         zcp[d].wait_recv()
         blk = cb.at[lax.rem(z + 8 - d, 8), x, c]
@@ -310,14 +311,20 @@
             gr[p, y] = gt[p, y]
     for cp in gcp:
         cp.wait_recv()
-    for i, d in enumerate(fo):
+    out_ref[...] = gr[...]
+
+    for cp in sends:
+        cp.wait_send()
+
+
+def place(gr_ref, c_ref, gram_ref, cross_ref):
+    z = lax.axis_index("tok") // 2
+    for i, d in enumerate(ARRIVAL):
         q = lax.rem(z + 8 - d, 8)
         for yy in range(8):
             o = pl.multiple_of((q * 2 + yy // 4) * 512 + yy % 4 * 128, 128)
-            gram_ref[:, pl.ds(o, 128)] = gr[i // 4, yy, :, i % 4 * 128:(i % 4 + 1) * 128].astype(F32)
-
-    for cp in sends:
-        cp.wait_send()
+            gram_ref[:, pl.ds(o, 128)] = gr_ref[i // 4, yy, :, i % 4 * 128:(i % 4 + 1) * 128].astype(F32)
+    cross_ref[...] = c_ref[...]
 
 
 def on_device(resid_in, norm_gain, gate_weight, up_weight, down_weight, labels):
@@ -334,20 +341,20 @@
         pltpu.VMEM((8, 128), F32),
         pltpu.VMEM((7, 8, 128), F32),
         pltpu.VMEM((2, 8, 128), F32),
+        pltpu.VMEM((8, 2, 32, 768), F32),
         pltpu.VMEM((8, 2, 32, 1024), F32),
-        pltpu.VMEM((8, 2, 32, 768), F32),
+        pltpu.VMEM((4, 2, 2, 32, 768), BF16),
         pltpu.VMEM((4, 2, 2, 32, 1024), BF16),
         pltpu.VMEM((4, 2, 2, 32, 768), BF16),
         pltpu.VMEM((4, 2, 2, 32, 1024), BF16),
-        pltpu.VMEM((4, 2, 2, 32, 768), BF16),
+        pltpu.VMEM((2, 32, 768), F32),
         pltpu.VMEM((2, 32, 1024), F32),
-        pltpu.VMEM((2, 32, 768), F32),
+        pltpu.VMEM((2, 32, 768), BF16),
         pltpu.VMEM((2, 32, 1024), BF16),
         pltpu.VMEM((2, 32, 768), BF16),
         pltpu.VMEM((2, 32, 1024), BF16),
-        pltpu.VMEM((2, 32, 768), BF16),
+        pltpu.VMEM((8, 2, 32, 384), BF16),
         pltpu.VMEM((8, 2, 32, 512), BF16),
-        pltpu.VMEM((8, 2, 32, 384), BF16),
         pltpu.VMEM((4, 4, 2, 16, 512), F32),
         pltpu.VMEM((4, 4, 16, 512), BF16),
         pltpu.VMEM((4, 4, 16, 512), BF16),
@@ -369,15 +376,21 @@
         dma((19,)), dma((19,)),
         dma((61,)), dma((61,)),
     ]
-    return pl.pallas_call(
+    pieces, cross = pl.pallas_call(
         kernel,
-        out_shape=(jax.ShapeDtypeStruct((16, 8192), F32), jax.ShapeDtypeStruct((16, CLASSES), F32)),
+        out_shape=(jax.ShapeDtypeStruct((2, 8, 16, 512), BF16), jax.ShapeDtypeStruct((16, CLASSES), F32)),
         in_specs=[vm, vm, hbm, hbm, hbm, vm],
         out_specs=(vm, vm),
         scratch_shapes=scratch,
         compiler_params=pltpu.CompilerParams(
             collective_id=0, has_side_effects=True, vmem_limit_bytes=60 * 2**20),
     )(resid_in, norm_gain.reshape(1, -1), gate_weight, up_weight, down_weight, labels.reshape(1, -1))
+    return pl.pallas_call(
+        place,
+        out_shape=(jax.ShapeDtypeStruct((16, 8192), F32), jax.ShapeDtypeStruct((16, CLASSES), F32)),
+        in_specs=[vm, vm],
+        out_specs=(vm, vm),
+    )(pieces, cross)
 
 
 def solution(mesh):

time: 103 us -> 100 us (0.971)
  local copies, waits for them, and re-layouts: 2.48 us -> 0 us
    unnamed x4 -> x0, local copies, waits for them, and re-layouts: 2.48 us -> none
    pallas_call x1 -> x2, Pallas kernels: 99.5 us -> 99.2 us  [the longest x1 97.4 us: on_device(): pl.pallas_call(kernel, out_shape=(jax.ShapeDtypeStruct((2, 8, 16, 512), B...]
where the time goes in v4:
time: 100 us; the launch traced here: 99.9 us
  Pallas kernels  99.2 us (99%)
    pallas_call x1, Pallas kernels, on_device(): pl.pallas_call(kernel, out_shape=(jax.ShapeDtypeStruct((2, 8, 16, 512), B...  97.4 us

profile of v4, /device:TPU:1, one launch (start us, length us, event | category | flops | bytes accessed | tf_op | source)
XLA Modules:
  0.0 99.9 jit_solution(5790227911484653109)
XLA Ops:
  0.6 97.4 %shard_map.77 = (bf16[2,8,16,512]{3,2,1,0:T(8,128)(2,1)}, f32[16,64]{1,0:T(8,128)}) custom-call(bf16[16,512]{1,0:T(8,128)(2,1)} %x_ref.1, f32[1,512]{1,0:T(1,128)} %bitcast.2, bf16[512,896]{1,0:T(8,128)(2,1)} %wg_hbm.1, bf16[512,896]{1,0:T(8,128)(2,1)} %wu_hbm.1, bf16[896,512]{1,0:T(8,128)(2,1)} %wd_hbm.1, s32[1,512]{1,0:T(1,128)} %bitcast.3), custom_call_target="tpu_custom_call" | custom-call | tf_op jit(solution)/shard_map/pallas_call | solution.py:379
  98.0 1.8 %shard_map.78 = (f32[16,8192]{1,0:T(8,128)}, f32[16,64]{1,0:T(8,128)}) custom-call(bf16[2,8,16,512]{3,2,1,0:T(8,128)(2,1)} %get-tuple-element.4.gr_ref, f32[16,64]{1,0:T(8,128)} %get-tuple-element.5.c_ref), custom_call_target="tpu_custom_call" | custom-call | tf_op jit(solution)/shard_map/pallas_call | solution.py:388
